TPU v7x, 128 devices: a whole 4x4x4 slice. The times are simulated.
128 devices in a mesh: term: 32 (over y_lo, x, z), pair: 4 (over y_hi, core).
Axes of the slice: x: 4, y: 4 (y_hi: 2, y_lo: 2; y = y_hi * 2 + y_lo), z: 4, core: 2. Of those that a mesh axis runs over, the one named last changes fastest.
Arguments:
- core_rows: bfloat16 [12288, 256], P(('term', 'pair')), may hold values from -0.25 to 0.25
- norm_ops: bfloat16 [2048, 512, 512], P(('term', 'pair')), may hold values from -6 to 6
- norm_sectors: int32 [2048, 2], P(('term', 'pair')), may hold values from 0 to 23
- comp_ops: bfloat16 [2048, 512, 512], P(('term', 'pair')), may hold values from -1.5 to 1.5
- comp_sectors: int32 [2048, 2], P(('term', 'pair')), may hold values from 0 to 23
- comp_group: int32 [2048, 1], P(('term', 'pair')), may hold values from 0 to 3; in each aligned block of 16 rows (0 to 15, 16 to 31, ...) at most 8 rows name the same one
- comp_slot: int32 [2048], P(('term', 'pair')), may hold values from 0 to 31
Outputs:
- normal_rotated: bfloat16 [2048, 256, 256], P(('term', 'pair'))
- comp_rotated: bfloat16 [4, 32, 256, 256], P('pair', 'term')
Inputs may be any that keep to these rules, and one draw needn't show every extreme that they name: `comp_group`: among the complementary tiles of one device (aligned blocks of 16 rows), at most 8 name the same owner group, a bound that some block reaches of them.
All inputs are finite; a program needn't handle non-finite values.
Results may differ from a plain program's by a relative error of at most 0.017.
Values may be sent and summed in bfloat16 or wider, within the bound.
No kernel may reach another device: no remote copies, remote signals or barrier semaphores. Data moves between devices by JAX's collectives and lax.ppermute only.
A program may use at most 128 MiB of HBM per device.

v0:
```python
import jax
import jax.numpy as jnp
from jax import lax
from jax.sharding import PartitionSpec as P

PAIR_DEV = 1


def rotate_tiles(core_tiles, op_tiles, sector_ids):
    left_rot = core_tiles[sector_ids[:, 0]]
    right_rot = core_tiles[sector_ids[:, 1]]
    half_rotated = jnp.einsum(
        "nab,nbc->nac", op_tiles, right_rot, preferred_element_type=jnp.float32
    ).astype(jnp.bfloat16)
    return jnp.einsum("nba,nbc->nac", left_rot, half_rotated, preferred_element_type=jnp.float32)


def on_device(core_rows, norm_ops, norm_sectors, comp_ops, comp_sectors, comp_group, comp_slot):
    tile_width = core_rows.shape[1]
    row_width = norm_ops.shape[1]
    gathered = lax.all_gather(core_rows, ("term", "pair"), axis=0, tiled=True)
    core_tiles = gathered.reshape(-1, row_width, tile_width)
    normal_rotated = rotate_tiles(core_tiles, norm_ops, norm_sectors).astype(jnp.bfloat16)
    groups = lax.axis_size("pair")
    term_count = lax.axis_size("term")
    comp_count = comp_ops.shape[0]
    capacity = comp_count // 2
    owned_slots = PAIR_DEV * term_count
    group_ids = comp_group[:, 0]
    member = (group_ids[:, None] == jnp.arange(groups, dtype=jnp.int32)[None, :]).astype(jnp.int32)
    before = jnp.cumsum(member, axis=0) - member
    target = group_ids * capacity + jnp.sum(before * member, axis=1)
    dispatch = target[None, :] == jnp.arange(groups * capacity, dtype=jnp.int32)[:, None]
    dispatch_bf = dispatch.astype(jnp.bfloat16)
    slots_out = (jnp.sum(jnp.where(dispatch, comp_slot[None, :] + 1, 0), axis=1) - 1).reshape(
        groups, capacity
    )
    rotated = (
        rotate_tiles(core_tiles, comp_ops, comp_sectors)
        .astype(jnp.bfloat16)
        .reshape(comp_count, -1)
    )
    outgoing = jnp.dot(dispatch_bf, rotated, preferred_element_type=jnp.float32)
    outgoing = outgoing.astype(jnp.bfloat16).reshape(groups, capacity, tile_width * tile_width)
    received, slots_in = (
        lax.all_to_all(outgoing, "pair", split_axis=0, concat_axis=0, tiled=True),
        lax.all_to_all(slots_out, "pair", split_axis=0, concat_axis=0, tiled=True),
    )
    select = (slots_in.reshape(1, -1) == jnp.arange(owned_slots, dtype=jnp.int32)[:, None]).astype(
        jnp.bfloat16
    )
    partial_value = jnp.dot(
        select, received.reshape(-1, tile_width * tile_width), preferred_element_type=jnp.float32
    )
    partial_bf = partial_value.astype(jnp.bfloat16)
    owned_sums = lax.psum_scatter(
        partial_bf.astype(jnp.float32).astype(jnp.bfloat16), "term", scatter_dimension=0, tiled=True
    )
    comp_rotated = owned_sums.reshape(1, PAIR_DEV, tile_width, tile_width)
    return (normal_rotated, comp_rotated)


def solution(mesh):
    return jax.shard_map(
        on_device,
        mesh=mesh,
        in_specs=(
            P(("term", "pair"), None),
            P(("term", "pair"), None, None),
            P(("term", "pair"), None),
            P(("term", "pair"), None, None),
            P(("term", "pair"), None),
            P(("term", "pair"), None),
            P(("term", "pair")),
        ),
        out_specs=(P(("term", "pair"), None, None), P("pair", "term", None, None)),
        check_vma=False,
    )
```

profile of v0, /device:TPU:0, one launch (start us, length us, event | category | flops | bytes accessed | tf_op | source)
XLA Modules:
  0.0 625.8 jit_solution(5890029725378413766)
XLA Ops:
  7.2 0.0 all-gather.2.cloned.1.call-start
  7.2 0.7 all-gather.2.cloned.1.call-update
  7.9 0.7 fusion.17
  8.7 0.8 select_reduce_fusion.1
  9.5 0.7 multiply_add_fusion
  10.2 0.1 select_reduce_fusion
  10.3 0.7 sub.11
  10.9 4.6 all-to-all-start
  15.5 0.8 fusion.22
  16.3 195.9 %all-gather.2.cloned.1.call-done = bf16[12288,256]{1,0:T(8,128)(2,1)} async-done(((bf16[96,256]{1,0:T(8,128)(2,1)}), bf16[12288,256]{1,0:T(8,128)(2,1)}) %all-gather.2.cloned.1.call-update) | async-done | bytes 6291472 | tf_op jit(solution)/shard_map/all_gather | solution.py:21
  212.2 5.6 gather_fusion.2
  217.8 5.7 gather_fusion.3
  223.5 7.8 %fusion.13 = bf16[16,256,256]{2,1,0:T(8,128)(2,1)S(1)} fusion(bf16[16,512,256]{2,1,0:T(8,128)(2,1)} %gather_fusion.2, bf16[16,512,256]{2,1,0:T(8,128)(2,1)} %gather_fusion.3, bf16[16,512,512]{2,1,0:T(8,128)(2,1)} %param.10), kind=kOutput, calls=%fused_computation.15 | convolution fusion | flops 3224371200 | bytes 18874368 | tf_op jit(solution)/shard_map/nba,nbc->nac/dot_general | solution.py:15
  231.3 1.2 copy.25
  232.5 3.4 fusion
  235.8 0.0 all-to-all-done
  235.9 4.8 all-to-all-start.1
  240.7 0.0 all-reduce.3.cloned.1.call-start
  240.8 0.5 broadcast.80
  241.3 0.7 reduce.5
  241.9 0.1 eq.47
  242.0 48.4 %all-to-all-done.1 = bf16[4,8,65536]{2,1,0:T(8,128)(2,1)} async-done(((bf16[4,8,65536]{2,1,0:T(8,128)(2,1)}), bf16[4,8,65536]{2,1,0:T(8,128)(2,1)}, u32[]{:S(2)}, u32[]{:S(2)}) %all-to-all-start.1) | async-done | bytes 4194336 | tf_op jit(solution)/shard_map/all_to_all | solution.py:46
  290.4 5.5 convolution_convert_fusion
  295.9 0.0 copy-start.1
  295.9 0.0 copy-start
  295.9 0.0 all-reduce.3.cloned.1.call-update
  295.9 0.6 copy-done.1
  296.5 0.6 dynamic-slice
  297.1 0.0 copy-done
  297.1 5.6 gather_fusion.1
  302.7 5.6 gather_fusion
  308.3 8.8 %fusion.10 = bf16[16,256,256]{2,1,0:T(8,128)(2,1)} fusion(bf16[16,512,256]{2,1,0:T(8,128)(2,1)} %gather_fusion, bf16[16,512,256]{2,1,0:T(8,128)(2,1)} %gather_fusion.1, bf16[16,512,512]{2,1,0:T(8,128)(2,1)} %param.8), kind=kOutput, calls=%fused_computation.14 | convolution fusion | flops 3224371200 | bytes 18874368 | tf_op jit(solution)/shard_map/nba,nbc->nac/dot_general | solution.py:15
  317.2 298.4 %all-reduce.3.cloned.1.call-done = bf16[32,65536]{1,0:T(8,128)(2,1)} async-done(((bf16[32,65536]{1,0:T(8,128)(2,1)}), bf16[32,65536]{1,0:T(8,128)(2,1)}) %all-reduce.3.cloned.1.call-update) | async-done | bytes 4194320
  615.6 2.7 dynamic-slice_reduce_fusion
  618.3 0.7 reshape.52
  (5 shorter events, 0.1 us)
Async XLA Ops:
  7.2 205.0 %all-gather.2.cloned.1.call-start = ((), (), s32[]{:S(2)}) async-start(), calls=%async_computation.2 | async-start | bytes 6340608 | tf_op jit(solution)/shard_map/all_gather | solution.py:21
  10.9 224.9 %all-to-all-start = ((s32[4,1,8]{2,1,0:T(1,128)}), s32[4,1,8]{2,1,0:T(1,128)S(1)}, u32[]{:S(2)}, u32[]{:S(2)}) async-start(s32[4,1,8]{2,1,0:T(1,128)} %bitcast.4), calls=%async_computation | async-start | bytes 4096 | tf_op jit(solution)/shard_map/all_to_all | solution.py:47
  235.9 54.6 %all-to-all-start.1 = ((bf16[4,8,65536]{2,1,0:T(8,128)(2,1)}), bf16[4,8,65536]{2,1,0:T(8,128)(2,1)}, u32[]{:S(2)}, u32[]{:S(2)}) async-start(bf16[4,8,65536]{2,1,0:T(8,128)(2,1)} %fusion), calls=%async_computation.1 | async-start | bytes 8388608 | tf_op jit(solution)/shard_map/all_to_all | solution.py:46
  240.7 374.9 %all-reduce.3.cloned.1.call-start = ((), (), s32[]{:S(2)}) async-start(), calls=%async_computation.3 | async-start | bytes 8388608
  295.9 0.7 copy-start.1
  295.9 1.2 copy-start
Sparse Core Ops, SparseCore 0:
  9.7 202.4 all-gather.1
  296.0 319.5 all-reduce.2
where the time goes:
time: 626 us
  waiting for transfers between devices  543 us (87%)
  local copies, waits for them, and re-layouts  29.5 us (5%)
  matrix products  25.5 us (4%)
  between operations  14.1 us (2%)
  starting transfers between devices  9.5 us (2%)
    unnamed x3, waiting for transfers between devices  299 us
    all_gather x1, waiting for transfers between devices, on_device(): gathered = lax.all_gather(core_rows, ('term', 'pair'), axis=0, tiled=True)  196 us
    all_to_all x1, waiting for transfers between devices, on_device(): lax.all_to_all(outgoing, 'pair', split_axis=0, concat_axis=0, tiled=True)  48.4 us
    dot_general x2, matrix products, rotate_tiles(): jnp.einsum('nba,nbc->nac', left_rot, half_rotated, preferred_element_type...  16.7 us
  transfers between devices with their start and end apart: 4, of which 3 were waited for; matrix products, arithmetic and copies ran while one was open for 8% of the time, Pallas kernels for 0%

commit v1 on v0

--- a/solution.py
+++ b/solution.py
@@ -18,7 +18,12 @@
 def on_device(core_rows, norm_ops, norm_sectors, comp_ops, comp_sectors, comp_group, comp_slot):
     tile_width = core_rows.shape[1]
     row_width = norm_ops.shape[1]
-    gathered = lax.all_gather(core_rows, ("term", "pair"), axis=0, tiled=True)
+    gathered = jnp.concatenate(
+        lax.all_to_all(
+            jnp.stack([core_rows] * lax.axis_size(("term", "pair"))), ("term", "pair"), 0, 0
+        ),
+        axis=0,
+    )
     core_tiles = gathered.reshape(-1, row_width, tile_width)
     normal_rotated = rotate_tiles(core_tiles, norm_ops, norm_sectors).astype(jnp.bfloat16)
     groups = lax.axis_size("pair")

time: 626 us -> 525 us (0.84)
  waiting for transfers between devices: 543 us -> 429 us
  starting transfers between devices: 9.5 us -> 21.3 us
    all_gather x1 -> x0, waiting for transfers between devices: 196 us -> none  [on_device(): gathered = lax.all_gather(core_rows, ('term', 'pair'), axis=0, tiled=True)]
    all_to_all x0 -> x1, waiting for transfers between devices: none -> 78.4 us  [on_device(): lax.all_to_all(jnp.stack([core_rows] * lax.axis_size(('term', 'pair'))),...]
    all_to_all x0 -> x1, starting transfers between devices: none -> 11.6 us  [on_device(): lax.all_to_all(jnp.stack([core_rows] * lax.axis_size(('term', 'pair'))),...]
    unnamed x3 -> x2, waiting for transfers between devices: 299 us -> 302 us
  transfers between devices with their start and end apart: 4 -> 4, of which waited for: 3 -> 3; matrix products, arithmetic and copies ran while one was open for 8% -> 9% of each run, Pallas kernels for 0% -> 0%
where the time goes in v1:
time: 525 us
  waiting for transfers between devices  429 us (82%)
  local copies, waits for them, and re-layouts  33.8 us (6%)
  matrix products  25.4 us (5%)
  starting transfers between devices  21.3 us (4%)
  between operations  14.1 us (3%)
    unnamed x2, waiting for transfers between devices  302 us
    all_to_all x1, waiting for transfers between devices, on_device(): lax.all_to_all(jnp.stack([core_rows] * lax.axis_size(('term', 'pair'))),...  78.4 us
    all_to_all x1, waiting for transfers between devices, on_device(): lax.all_to_all(outgoing, 'pair', split_axis=0, concat_axis=0, tiled=True)  48.4 us
    dot_general x2, matrix products, rotate_tiles(): jnp.einsum('nba,nbc->nac', left_rot, half_rotated, preferred_element_type...  16.6 us
    all_to_all x1, starting transfers between devices, on_device(): lax.all_to_all(jnp.stack([core_rows] * lax.axis_size(('term', 'pair'))),...  11.6 us
    gather x2, local copies, waits for them, and re-layouts, rotate_tiles(): right_rot = core_tiles[sector_ids[:, 1]]  11.3 us
    gather x2, local copies, waits for them, and re-layouts, rotate_tiles(): left_rot = core_tiles[sector_ids[:, 0]]  11.2 us
  transfers between devices with their start and end apart: 4, of which 3 were waited for; matrix products, arithmetic and copies ran while one was open for 9% of the time, Pallas kernels for 0%

profile of v1, /device:TPU:0, one launch (start us, length us, event | category | flops | bytes accessed | tf_op | source)
XLA Modules:
  0.0 524.8 jit_solution(990809562243459844)
XLA Ops:
  7.2 4.2 stack.2
  11.4 0.0 copy-start
  11.4 0.0 copy-start.3
  11.4 0.0 copy-start.1
  11.4 11.6 %all-to-all-start = ((bf16[128,96,256]{2,1,0:T(8,128)(2,1)}), bf16[128,96,256]{2,1,0:T(8,128)(2,1)}, u32[]{:S(2)}, u32[]{:S(2)}) async-start(bf16[128,96,256]{2,1,0:T(8,128)(2,1)} %stack.2), calls=%async_computation | async-start | bytes 12582912 | tf_op jit(solution)/shard_map/all_to_all | solution.py:22
  23.1 0.0 copy-done
  23.1 0.1 fusion.17
  23.2 0.2 select_reduce_fusion.1
  23.4 0.0 copy-done.3
  23.4 0.1 select_reduce_fusion
  23.5 0.7 sub.11
  24.1 0.0 copy-done.1
  24.2 78.4 %all-to-all-done = bf16[128,96,256]{2,1,0:T(8,128)(2,1)} async-done(((bf16[128,96,256]{2,1,0:T(8,128)(2,1)}), bf16[128,96,256]{2,1,0:T(8,128)(2,1)}, u32[]{:S(2)}, u32[]{:S(2)}) %all-to-all-start) | async-done | bytes 6291488 | tf_op jit(solution)/shard_map/all_to_all | solution.py:22
  102.6 4.7 all-to-all-start.1
  107.3 5.6 %gather_fusion.2 = bf16[16,512,256]{2,1,0:T(8,128)(2,1)} fusion(bf16[24,512,256]{2,1,0:T(8,128)(2,1)} %bitcast, s32[1024]{0:T(1024)S(1)} %get-tuple-element.9), kind=kCustom, calls=%fused_computation.2 | custom fusion | bytes 8388672 | tf_op jit(solution)/shard_map/gather | solution.py:10
  113.0 5.7 %gather_fusion.3 = bf16[16,512,256]{2,1,0:T(8,128)(2,1)} fusion(bf16[24,512,256]{2,1,0:T(8,128)(2,1)} %bitcast, s32[1024]{0:T(1024)S(1)} %get-tuple-element.8), kind=kCustom, calls=%fused_computation.3 | custom fusion | bytes 8388672 | tf_op jit(solution)/shard_map/gather | solution.py:11
  118.6 7.8 %fusion.13 = bf16[16,256,256]{2,1,0:T(8,128)(2,1)S(1)} fusion(bf16[16,512,256]{2,1,0:T(8,128)(2,1)} %gather_fusion.2, bf16[16,512,256]{2,1,0:T(8,128)(2,1)} %gather_fusion.3, bf16[16,512,512]{2,1,0:T(8,128)(2,1)} %param.10), kind=kOutput, calls=%fused_computation.15 | convolution fusion | flops 3224371200 | bytes 18874368 | tf_op jit(solution)/shard_map/nba,nbc->nac/dot_general | solution.py:15
  126.4 1.2 copy.25
  127.6 3.4 fusion
  131.0 0.0 all-to-all-done.1
  131.0 4.8 all-to-all-start.2
  135.8 0.0 all-reduce.3.cloned.1.call-start
  135.9 0.5 broadcast.82
  136.4 0.7 reduce.5
  137.1 0.1 eq.47
  137.2 48.4 %all-to-all-done.2 = bf16[4,8,65536]{2,1,0:T(8,128)(2,1)} async-done(((bf16[4,8,65536]{2,1,0:T(8,128)(2,1)}), bf16[4,8,65536]{2,1,0:T(8,128)(2,1)}, u32[]{:S(2)}, u32[]{:S(2)}) %all-to-all-start.2) | async-done | bytes 4194336 | tf_op jit(solution)/shard_map/all_to_all | solution.py:51
  185.6 5.4 %convolution_convert_fusion = bf16[32,65536]{1,0:T(8,128)(2,1)} fusion(bf16[4,8,65536]{2,1,0:T(8,128)(2,1)} %all-to-all-done.2, s32[32]{0:T(128)S(1)} %eq.47), kind=kOutput, calls=%fused_computation.4 | convolution fusion | flops 136315904 | bytes 8388736 | tf_op jit(solution)/shard_map/dot_general | solution.py:57
  191.0 0.0 copy-start.4
  191.0 0.0 copy-start.2
  191.0 0.0 all-reduce.3.cloned.1.call-update
  191.0 0.6 copy-done.4
  191.7 0.6 dynamic-slice
  192.2 0.0 copy-done.2
  192.3 5.6 %gather_fusion.1 = bf16[16,512,256]{2,1,0:T(8,128)(2,1)} fusion(bf16[24,512,256]{2,1,0:T(8,128)(2,1)} %bitcast, s32[1024]{0:T(1024)S(1)} %get-tuple-element.6), kind=kCustom, calls=%fused_computation.1 | custom fusion | bytes 8388672 | tf_op jit(solution)/shard_map/gather | solution.py:11
  197.9 5.6 %gather_fusion = bf16[16,512,256]{2,1,0:T(8,128)(2,1)} fusion(bf16[24,512,256]{2,1,0:T(8,128)(2,1)} %bitcast, s32[1024]{0:T(1024)S(1)} %get-tuple-element.7), kind=kCustom, calls=%fused_computation | custom fusion | bytes 8388672 | tf_op jit(solution)/shard_map/gather | solution.py:10
  203.4 8.8 %fusion.10 = bf16[16,256,256]{2,1,0:T(8,128)(2,1)} fusion(bf16[16,512,256]{2,1,0:T(8,128)(2,1)} %gather_fusion, bf16[16,512,256]{2,1,0:T(8,128)(2,1)} %gather_fusion.1, bf16[16,512,512]{2,1,0:T(8,128)(2,1)} %param.8), kind=kOutput, calls=%fused_computation.14 | convolution fusion | flops 3224371200 | bytes 18874368 | tf_op jit(solution)/shard_map/nba,nbc->nac/dot_general | solution.py:15
  212.2 302.4 %all-reduce.3.cloned.1.call-done = bf16[32,65536]{1,0:T(8,128)(2,1)} async-done(((bf16[32,65536]{1,0:T(8,128)(2,1)}), bf16[32,65536]{1,0:T(8,128)(2,1)}) %all-reduce.3.cloned.1.call-update) | async-done | bytes 4194320
  514.6 2.7 dynamic-slice_reduce_fusion
  517.3 0.7 reshape.50
  (7 shorter events, 0.1 us)
Async XLA Ops:
  11.4 11.7 %copy-start = (s32[16,1]{0,1:T(1,128)S(1)}, s32[16,1]{0,1:T(1,128)}, u32[]{:S(2)}) copy-start(s32[16,1]{0,1:T(1,128)} %param.12) | copy-start | bytes 196
  11.4 12.0 %copy-start.3 = (s32[16]{0:T(128)S(1)}, s32[16]{0:T(128)}, u32[]{:S(2)}) copy-start(s32[16]{0:T(128)} %param.13) | copy-start | bytes 196
  11.4 12.7 %copy-start.1 = (s32[16,2]{0,1:T(2,128)S(1)}, s32[16,2]{0,1:T(2,128)}, u32[]{:S(2)}) copy-start(s32[16,2]{0,1:T(2,128)} %param.11) | copy-start | bytes 388
  11.4 91.2 %all-to-all-start = ((bf16[128,96,256]{2,1,0:T(8,128)(2,1)}), bf16[128,96,256]{2,1,0:T(8,128)(2,1)}, u32[]{:S(2)}, u32[]{:S(2)}) async-start(bf16[128,96,256]{2,1,0:T(8,128)(2,1)} %stack.2), calls=%async_computation | async-start | bytes 12582912 | tf_op jit(solution)/shard_map/all_to_all | solution.py:22
  102.6 28.4 %all-to-all-start.1 = ((s32[4,1,8]{2,1,0:T(1,128)}), s32[4,1,8]{2,1,0:T(1,128)S(1)}, u32[]{:S(2)}, u32[]{:S(2)}) async-start(s32[4,1,8]{2,1,0:T(1,128)} %bitcast.4), calls=%async_computation.1 | async-start | bytes 4096 | tf_op jit(solution)/shard_map/all_to_all | solution.py:52
  131.0 54.6 %all-to-all-start.2 = ((bf16[4,8,65536]{2,1,0:T(8,128)(2,1)}), bf16[4,8,65536]{2,1,0:T(8,128)(2,1)}, u32[]{:S(2)}, u32[]{:S(2)}) async-start(bf16[4,8,65536]{2,1,0:T(8,128)(2,1)} %fusion), calls=%async_computation.2 | async-start | bytes 8388608 | tf_op jit(solution)/shard_map/all_to_all | solution.py:51
  135.8 378.8 %all-reduce.3.cloned.1.call-start = ((), (), s32[]{:S(2)}) async-start(), calls=%async_computation.3 | async-start | bytes 8388608
  191.0 0.7 copy-start.4
  191.0 1.2 copy-start.2
Sparse Core Ops, SparseCore 0:
  191.1 323.4 all-reduce.2
